TPU v7x, 256 devices: a whole 4x4x8 slice. The times are simulated.
256 devices in a mesh: blk: 128 (over z, x, y), rep: 2 (over core).
Axes of the slice: x: 4, y: 4, z: 8, core: 2. Of those that a mesh axis runs over, the one named last changes fastest.
Arguments:
- hamiltonian: bfloat16 [1024, 7, 128, 128], P(('blk', 'rep')), may hold values from -0.7 to 0.7
- lists: int32 [1024, 4], P(('blk', 'rep')), may hold values from 0 to 1023, as said below
- scales: float32 [1024], P(('blk', 'rep')), may hold values from 0.8 to 1.2
- weights: float32 [1024, 4], P(('blk', 'rep')), may hold values from 0.25 to 1
Outputs:
- density: float32 [1024, 7, 128, 128], P(('blk', 'rep'))
Inputs may be any that keep to these rules, and one draw needn't show every extreme that they name: lists[j, 0] is j; the other entries of a row are distinct, differ from j, and lie within 3 blocks of j counted modulo 1024.
All inputs are finite; a program needn't handle non-finite values.
Results may differ from a plain program's by a relative error of at most 0.00096.
Values may be sent and summed in bfloat16 or wider, within the bound.
A program may use at most 64 MiB of HBM per device.

v0:
```python
import jax
import jax.numpy as jnp
from jax import lax
from jax.sharding import PartitionSpec as P

REACH = 3
ITERS = 5


def extended(block, sides, width):
    for axis, dim in sides:
        count = lax.axis_size(axis)
        forward = [(i, i + 1) for i in range(count - 1)]
        forward.append((count - 1, 0))
        backward = [(target, source) for source, target in forward]
        low = lax.ppermute(
            lax.slice_in_dim(block, block.shape[dim] - width, None, axis=dim), axis, forward
        )
        high = lax.ppermute(lax.slice_in_dim(block, 0, width, axis=dim), axis, backward)
        block = jnp.concatenate([low, block, high], axis=dim)
    return block


def passed_along(value, axis, steps):
    count = lax.axis_size(axis)
    pairs = [(source, (source + steps) % count) for source in range(count)]
    return lax.ppermute(value, axis, pairs)


def wrapped(delta, total):
    half_total = total // 2
    return (delta + half_total) % total - half_total


def assemble(blocks, valid):
    upper = jnp.where(valid[:, :, None, None], blocks.astype(jnp.float32), jnp.float32(0.0))
    both = 0.5 * (upper + jnp.transpose(upper, (1, 0, 3, 2)))
    count, width = (both.shape[0], both.shape[2])
    return jnp.transpose(both, (0, 2, 1, 3)).reshape(count * width, count * width)


def sign_density(matrix, scale):
    current = scale * matrix
    for step in range(ITERS):
        rounded = current.astype(jnp.bfloat16)
        square = jnp.dot(rounded, rounded, preferred_element_type=jnp.float32).astype(jnp.bfloat16)
        current = 1.5 * current - 0.5 * jnp.dot(rounded, square, preferred_element_type=jnp.float32)
    order = matrix.shape[0]
    return 0.5 * (jnp.eye(order, dtype=jnp.float32) - current)


def on_device(hamiltonian, lists, scales, weights):
    rows, band, width = (hamiltonian.shape[0], hamiltonian.shape[1], hamiltonian.shape[2])
    half_band = band // 2
    total = rows * lax.axis_size(("blk", "rep"))
    first = lax.axis_index(("blk", "rep")) * rows
    padded = extended(hamiltonian, ((("blk", "rep"), 0),), REACH)
    extent = rows + 2 * REACH

    def visit(accum, inputs):
        members, scale, share = inputs
        local = (members - first + REACH) % total
        offset = wrapped(members[None, :] - members[:, None], total)
        valid = jnp.abs(offset) <= half_band
        slot = jnp.clip(offset + half_band, 0, band - 1)
        blocks = padded[local[:, None], slot]
        density = sign_density(assemble(blocks, valid), scale)
        count = members.shape[0]
        pieces = jnp.transpose(density.reshape(count, width, count, width), (0, 2, 1, 3))
        pieces = jnp.where(
            valid[:, :, None, None], pieces * share[:, None, None, None], jnp.float32(0.0)
        )
        accum = accum.at[local[:, None], slot].add(pieces)
        return (accum, None)

    accum = jnp.zeros((extent, band, width, width), jnp.float32)
    accum, unused = lax.scan(visit, accum, (lists, scales, weights))
    from_left = passed_along(accum[rows + REACH :], ("blk", "rep"), 1)
    from_right = passed_along(accum[:REACH], ("blk", "rep"), -1)
    owned = accum[REACH : REACH + rows]
    owned = owned.at[:REACH].add(from_left)
    owned = owned.at[rows - REACH :].add(from_right)
    return owned


def solution(mesh):
    in_specs = (
        P(("blk", "rep"), None, None, None),
        P(("blk", "rep"), None),
        P(("blk", "rep")),
        P(("blk", "rep"), None),
    )
    out_specs = P(("blk", "rep"), None, None, None)
    return jax.shard_map(
        on_device, mesh=mesh, in_specs=in_specs, out_specs=out_specs, check_vma=False
    )
```

profile of v0, /device:TPU:0, one launch (start us, length us, event | category | flops | bytes accessed | tf_op | source)
XLA Modules:
  0.0 121.8 jit_solution(9778336384896759654)
XLA Ops:
  0.0 2.4 %fusion.39 = (bf16[3,7,128,128]{3,2,1,0:T(8,128)(2,1)}, bf16[3,7,128,128]{3,2,1,0:T(8,128)(2,1)S(1)}) fusion(bf16[4,7,128,128]{3,2,1,0:T(8,128)(2,1)} %param.10), kind=kLoop, calls=%fused_computation.73 | loop fusion | bytes 2752512 | tf_op jit(solution)/shard_map/slice | solution.py:17
  2.4 8.2 %collective-permute-start.1 = (bf16[3,7,128,128]{3,2,1,0:T(8,128)(2,1)S(1)}, bf16[3,7,128,128]{3,2,1,0:T(8,128)(2,1)S(1)}, u32[]{:S(2)}, u32[]{:S(2)}) collective-permute-start(bf16[3,7,128,128]{3,2,1,0:T(8,128)(2,1)S(1)} %get-tuple-element.199), channel_id=1, source_target_pairs={{1,0},{2,1},{3,2},{4,3},{5,4},{6,5},{7,6},{8,7},{9,8},{10,9},{11,1... | collective-permute-start | bytes 2064392 | tf_op jit(solution)/shard_map/ppermute | solution.py:19
  10.6 8.8 %collective-permute-done = bf16[3,7,128,128]{3,2,1,0:T(8,128)(2,1)S(1)} collective-permute-done((bf16[3,7,128,128]{3,2,1,0:T(8,128)(2,1)}, bf16[3,7,128,128]{3,2,1,0:T(8,128)(2,1)S(1)}, u32[]{:S(2)}, u32[]{:S(2)}) %collective-permute-start) | collective-permute-done | bytes 688160 | tf_op jit(solution)/shard_map/ppermute | solution.py:16
  19.4 1.7 %pad_maximum_fusion = bf16[10,7,128,128]{3,2,1,0:T(8,128)(2,1)} fusion(bf16[3,7,128,128]{3,2,1,0:T(8,128)(2,1)S(1)} %collective-permute-done.1, bf16[4,7,128,128]{3,2,1,0:T(8,128)(2,1)S(1)} %copy-done.1, bf16[3,7,128,128]{3,2,1,0:T(8,128)(2,1)S(1)} %collective-permute-done), kind=kLoop, calls=%fused_computation.68 | loop fusion | flops 2293760 | bytes 4587520 | tf_op jit(solution)/shard_map/concatenate | solution.py:20
  21.1 2.6 %broadcast_in_dim.61 = f32[10,7,128,128]{3,2,1,0:T(8,128)} broadcast(f32[]{:T(128)} %constant.205.clone.1), dimensions={} | broadcast | bytes 4587524 | tf_op jit(solution)/shard_map/broadcast_in_dim | solution.py:76
  23.7 68.7 %while.16 = (s32[]{:T(128)}, f32[10,7,128,128]{3,2,1,0:T(8,128)}, s32[4,4]{1,0:T(4,128)}, s32[]{:T(128)}, bf16[10,7,128,128]{3,2,1,0:T(8,128)(2,1)}, /*index=5*/...) while((s32[]{:T(128)}, f32[10,7,128,128]{3,2,1,0:T(8,128)}, s32[4,4]{1,0:T(4,128)}, s32[]{:T(128)}, ...), condition=%wide.region_2.3_spmd, body=%wide.region_0.2_spmd.sunk | while | flops 2695103488 | bytes 28312596 | solution.py:77
  23.7 0.6 dynamic_slice.36
  25.0 0.7 dynamic-slice_bitcast_fusion.4
  25.7 0.7 clamp_shift-left_fusion.3
  26.7 2.3 %gather_fusion = bf16[16,128,128]{2,1,0:T(8,128)(2,1)S(1)} fusion(bf16[10,7,128,128]{3,2,1,0:T(8,128)(2,1)} %get-tuple-element.283, s32[16]{0:T(128)S(1)} %reshape.322), kind=kCustom, calls=%fused_computation.clone.1 | custom fusion | bytes 1048704 | tf_op jit(solution)/shard_map/while/body/eval_jaxpr/gather | solution.py:66
  29.1 0.3 copy.35
  29.4 2.0 %fusion.70 = (bf16[4,128,4,128]{3,2,1,0:T(4,128)(2,1)S(1)}, f32[4,128,4,128]{3,2,1,0:T(4,128)}) fusion(f32[]{:T(128)} %bitcast.60, f32[4,4,128,128]{2,0,3,1:T(4,128)S(1)} %copy.35, pred[4,4]{1,0:T(4,128)(4,1)S(1)} %get-tuple-element.257, f32[4,4,128,128]{3,2,1,0:T(8,128)S(1)} %convert.12, pred[4,4]{1,0:T(4,128)(4,1)S(1)} %get-tuple-element.258), kind=kLoop, calls=%fused_computation.67.clone.1 | loop fusion | flops 1572864 | bytes 3670052 | tf_op jit(solution)/shard_map/while/body/eval_jaxpr/convert_element_type | solution.py:45
  31.4 2.0 %fusion.71 = f32[512,512]{1,0:T(8,128)S(1)} fusion(f32[64,8,4,128]{3,2,1,0:T(4,128)} %bitcast.68, bf16[64,8,4,128]{3,2,1,0:T(4,128)(2,1)S(1)} %bitcast.69), kind=kOutput, calls=%fused_computation.13.clone.1 | convolution fusion | flops 537657344 | bytes 2621440 | tf_op jit(solution)/shard_map/while/body/eval_jaxpr/dot_general | solution.py:47
  33.4 0.8 fusion.72
  34.2 0.8 fusion.73
  35.0 0.8 fusion.74
  35.8 0.8 fusion.75
  36.6 0.4 reshape.323
  37.0 0.3 select_bitcast_fusion.2
  37.4 3.5 %scatter_fusion = f32[10,7,128,128]{3,2,1,0:T(8,128)} fusion(f32[10,7,128,128]{3,2,1,0:T(8,128)} %get-tuple-element.271, s32[16]{0:T(128)S(1)} %reshape.321, f32[16,128,128]{2,1,0:T(8,128)S(1)} %bitcast.67), kind=kCustom, calls=%fused_computation.1.clone.1 | custom fusion | flops 262144 | bytes 3145856 | tf_op jit(solution)/shard_map/while/body/eval_jaxpr/scatter-add | solution.py:73
  40.9 0.6 dynamic_slice.36
  42.2 0.7 dynamic-slice_bitcast_fusion.4
  42.8 0.7 clamp_shift-left_fusion.3
  43.9 2.3 %gather_fusion = bf16[16,128,128]{2,1,0:T(8,128)(2,1)S(1)} fusion(bf16[10,7,128,128]{3,2,1,0:T(8,128)(2,1)} %get-tuple-element.283, s32[16]{0:T(128)S(1)} %reshape.322), kind=kCustom, calls=%fused_computation.clone.1 | custom fusion | bytes 1048704 | tf_op jit(solution)/shard_map/while/body/eval_jaxpr/gather | solution.py:66
  46.6 2.0 %fusion.70 = (bf16[4,128,4,128]{3,2,1,0:T(4,128)(2,1)S(1)}, f32[4,128,4,128]{3,2,1,0:T(4,128)}) fusion(f32[]{:T(128)} %bitcast.60, f32[4,4,128,128]{2,0,3,1:T(4,128)S(1)} %copy.35, pred[4,4]{1,0:T(4,128)(4,1)S(1)} %get-tuple-element.257, f32[4,4,128,128]{3,2,1,0:T(8,128)S(1)} %convert.12, pred[4,4]{1,0:T(4,128)(4,1)S(1)} %get-tuple-element.258), kind=kLoop, calls=%fused_computation.67.clone.1 | loop fusion | flops 1572864 | bytes 3670052 | tf_op jit(solution)/shard_map/while/body/eval_jaxpr/convert_element_type | solution.py:45
  48.6 2.0 %fusion.71 = f32[512,512]{1,0:T(8,128)S(1)} fusion(f32[64,8,4,128]{3,2,1,0:T(4,128)} %bitcast.68, bf16[64,8,4,128]{3,2,1,0:T(4,128)(2,1)S(1)} %bitcast.69), kind=kOutput, calls=%fused_computation.13.clone.1 | convolution fusion | flops 537657344 | bytes 2621440 | tf_op jit(solution)/shard_map/while/body/eval_jaxpr/dot_general | solution.py:47
  50.6 0.8 fusion.72
  51.4 0.8 fusion.73
  52.2 0.8 fusion.74
  53.0 0.8 fusion.75
  53.8 0.4 reshape.323
  54.2 0.3 select_bitcast_fusion.2
  54.6 3.4 %scatter_fusion = f32[10,7,128,128]{3,2,1,0:T(8,128)} fusion(f32[10,7,128,128]{3,2,1,0:T(8,128)} %get-tuple-element.271, s32[16]{0:T(128)S(1)} %reshape.321, f32[16,128,128]{2,1,0:T(8,128)S(1)} %bitcast.67), kind=kCustom, calls=%fused_computation.1.clone.1 | custom fusion | flops 262144 | bytes 3145856 | tf_op jit(solution)/shard_map/while/body/eval_jaxpr/scatter-add | solution.py:73
  58.1 0.6 dynamic_slice.36
  59.3 0.7 dynamic-slice_bitcast_fusion.4
  60.0 0.7 clamp_shift-left_fusion.3
  61.0 2.3 %gather_fusion = bf16[16,128,128]{2,1,0:T(8,128)(2,1)S(1)} fusion(bf16[10,7,128,128]{3,2,1,0:T(8,128)(2,1)} %get-tuple-element.283, s32[16]{0:T(128)S(1)} %reshape.322), kind=kCustom, calls=%fused_computation.clone.1 | custom fusion | bytes 1048704 | tf_op jit(solution)/shard_map/while/body/eval_jaxpr/gather | solution.py:66
  63.7 2.0 %fusion.70 = (bf16[4,128,4,128]{3,2,1,0:T(4,128)(2,1)S(1)}, f32[4,128,4,128]{3,2,1,0:T(4,128)}) fusion(f32[]{:T(128)} %bitcast.60, f32[4,4,128,128]{2,0,3,1:T(4,128)S(1)} %copy.35, pred[4,4]{1,0:T(4,128)(4,1)S(1)} %get-tuple-element.257, f32[4,4,128,128]{3,2,1,0:T(8,128)S(1)} %convert.12, pred[4,4]{1,0:T(4,128)(4,1)S(1)} %get-tuple-element.258), kind=kLoop, calls=%fused_computation.67.clone.1 | loop fusion | flops 1572864 | bytes 3670052 | tf_op jit(solution)/shard_map/while/body/eval_jaxpr/convert_element_type | solution.py:45
  65.7 2.0 %fusion.71 = f32[512,512]{1,0:T(8,128)S(1)} fusion(f32[64,8,4,128]{3,2,1,0:T(4,128)} %bitcast.68, bf16[64,8,4,128]{3,2,1,0:T(4,128)(2,1)S(1)} %bitcast.69), kind=kOutput, calls=%fused_computation.13.clone.1 | convolution fusion | flops 537657344 | bytes 2621440 | tf_op jit(solution)/shard_map/while/body/eval_jaxpr/dot_general | solution.py:47
  67.8 0.8 fusion.72
  68.5 0.8 fusion.73
  69.3 0.8 fusion.74
  70.1 0.8 fusion.75
  71.0 0.4 reshape.323
  71.3 0.3 select_bitcast_fusion.2
  71.8 3.5 %scatter_fusion = f32[10,7,128,128]{3,2,1,0:T(8,128)} fusion(f32[10,7,128,128]{3,2,1,0:T(8,128)} %get-tuple-element.271, s32[16]{0:T(128)S(1)} %reshape.321, f32[16,128,128]{2,1,0:T(8,128)S(1)} %bitcast.67), kind=kCustom, calls=%fused_computation.1.clone.1 | custom fusion | flops 262144 | bytes 3145856 | tf_op jit(solution)/shard_map/while/body/eval_jaxpr/scatter-add | solution.py:73
  75.3 0.6 dynamic_slice.36
  76.5 0.7 dynamic-slice_bitcast_fusion.4
  77.2 0.7 clamp_shift-left_fusion.3
  78.2 2.3 %gather_fusion = bf16[16,128,128]{2,1,0:T(8,128)(2,1)S(1)} fusion(bf16[10,7,128,128]{3,2,1,0:T(8,128)(2,1)} %get-tuple-element.283, s32[16]{0:T(128)S(1)} %reshape.322), kind=kCustom, calls=%fused_computation.clone.1 | custom fusion | bytes 1048704 | tf_op jit(solution)/shard_map/while/body/eval_jaxpr/gather | solution.py:66
  81.0 2.0 %fusion.70 = (bf16[4,128,4,128]{3,2,1,0:T(4,128)(2,1)S(1)}, f32[4,128,4,128]{3,2,1,0:T(4,128)}) fusion(f32[]{:T(128)} %bitcast.60, f32[4,4,128,128]{2,0,3,1:T(4,128)S(1)} %copy.35, pred[4,4]{1,0:T(4,128)(4,1)S(1)} %get-tuple-element.257, f32[4,4,128,128]{3,2,1,0:T(8,128)S(1)} %convert.12, pred[4,4]{1,0:T(4,128)(4,1)S(1)} %get-tuple-element.258), kind=kLoop, calls=%fused_computation.67.clone.1 | loop fusion | flops 1572864 | bytes 3670052 | tf_op jit(solution)/shard_map/while/body/eval_jaxpr/convert_element_type | solution.py:45
  82.9 2.0 %fusion.71 = f32[512,512]{1,0:T(8,128)S(1)} fusion(f32[64,8,4,128]{3,2,1,0:T(4,128)} %bitcast.68, bf16[64,8,4,128]{3,2,1,0:T(4,128)(2,1)S(1)} %bitcast.69), kind=kOutput, calls=%fused_computation.13.clone.1 | convolution fusion | flops 537657344 | bytes 2621440 | tf_op jit(solution)/shard_map/while/body/eval_jaxpr/dot_general | solution.py:47
  85.0 0.8 fusion.72
  85.8 0.8 fusion.73
  86.5 0.8 fusion.74
  87.3 0.8 fusion.75
  88.2 0.4 reshape.323
  88.5 0.3 select_bitcast_fusion.2
  89.0 3.5 %scatter_fusion = f32[10,7,128,128]{3,2,1,0:T(8,128)} fusion(f32[10,7,128,128]{3,2,1,0:T(8,128)} %get-tuple-element.271, s32[16]{0:T(128)S(1)} %reshape.321, f32[16,128,128]{2,1,0:T(8,128)S(1)} %bitcast.67), kind=kCustom, calls=%fused_computation.1.clone.1 | custom fusion | flops 262144 | bytes 3145856 | tf_op jit(solution)/shard_map/while/body/eval_jaxpr/scatter-add | solution.py:73
  92.4 2.1 %fusion.38 = (f32[3,7,128,128]{3,2,1,0:T(8,128)S(1)}, f32[3,7,128,128]{3,2,1,0:T(8,128)S(1)}) fusion(f32[10,7,128,128]{3,2,1,0:T(8,128)} %get-tuple-element.172), kind=kLoop, calls=%fused_computation.72 | loop fusion | bytes 5505024 | tf_op jit(solution)/shard_map/slice | solution.py:79
  94.6 7.2 %collective-permute-start.3 = (f32[3,7,128,128]{3,2,1,0:T(8,128)S(1)}, f32[3,7,128,128]{3,2,1,0:T(8,128)S(1)}, u32[]{:S(2)}, u32[]{:S(2)}) collective-permute-start(f32[3,7,128,128]{3,2,1,0:T(8,128)S(1)} %get-tuple-element.196), channel_id=1, source_target_pairs={{0,255},{1,0},{2,1},{3,2},{4,3},{5,4},{6,5},{7,6},{8,7},{9,8},{10,... | collective-permute-start | bytes 4128776 | tf_op jit(solution)/shard_map/ppermute | solution.py:27
  102.0 15.8 %collective-permute-done.2 = f32[3,7,128,128]{3,2,1,0:T(8,128)S(1)} collective-permute-done((f32[3,7,128,128]{3,2,1,0:T(8,128)S(1)}, f32[3,7,128,128]{3,2,1,0:T(8,128)S(1)}, u32[]{:S(2)}, u32[]{:S(2)}) %collective-permute-start.2) | collective-permute-done | bytes 1376288 | tf_op jit(solution)/shard_map/ppermute | solution.py:27
  118.0 1.2 copy-done.2
  119.2 2.6 %fusion.37 = f32[4,7,128,128]{3,2,1,0:T(8,128)} fusion(f32[4,7,128,128]{3,2,1,0:T(8,128)} %copy-done.2, f32[3,7,128,128]{3,2,1,0:T(8,128)S(1)} %collective-permute-done.3), kind=kLoop, calls=%fused_computation.70 | loop fusion | flops 344064 | bytes 4128768 | tf_op jit(solution)/shard_map/scatter-add | solution.py:82
  (44 shorter events, 3.6 us)
Async XLA Ops:
  0.0 19.4 %copy-start.1 = (bf16[4,7,128,128]{3,2,1,0:T(8,128)(2,1)S(1)}, bf16[4,7,128,128]{3,2,1,0:T(8,128)(2,1)}, u32[]{:S(2)}) copy-start(bf16[4,7,128,128]{3,2,1,0:T(8,128)(2,1)} %param.10) | copy-start | bytes 2752516
  2.4 17.0 %collective-permute-start = (bf16[3,7,128,128]{3,2,1,0:T(8,128)(2,1)}, bf16[3,7,128,128]{3,2,1,0:T(8,128)(2,1)S(1)}, u32[]{:S(2)}, u32[]{:S(2)}) collective-permute-start(bf16[3,7,128,128]{3,2,1,0:T(8,128)(2,1)} %get-tuple-element.198), channel_id=1, source_target_pairs={{0,1},{1,2},{2,3},{3,4},{4,5},{5,6},{6,7},{7,8},{8,9},{9,10},{10,1... | collective-permute-start | bytes 2064392 | tf_op jit(solution)/shard_map/ppermute | solution.py:16
  2.4 17.0 %collective-permute-start.1 = (bf16[3,7,128,128]{3,2,1,0:T(8,128)(2,1)S(1)}, bf16[3,7,128,128]{3,2,1,0:T(8,128)(2,1)S(1)}, u32[]{:S(2)}, u32[]{:S(2)}) collective-permute-start(bf16[3,7,128,128]{3,2,1,0:T(8,128)(2,1)S(1)} %get-tuple-element.199), channel_id=1, source_target_pairs={{1,0},{2,1},{3,2},{4,3},{5,4},{6,5},{7,6},{8,7},{9,8},{10,9},{11,1... | collective-permute-start | bytes 2064392 | tf_op jit(solution)/shard_map/ppermute | solution.py:19
  21.1 2.6 %copy-start.3 = (f32[4]{0:T(128)S(1)}, f32[4]{0:T(128)}, u32[]{:S(2)}) copy-start(f32[4]{0:T(128)} %param.12) | copy-start | bytes 52
  92.4 9.3 %copy-start = (f32[10,7,128,128]{3,2,1,0:T(8,128)S(1)}, f32[10,7,128,128]{3,2,1,0:T(8,128)}, u32[]{:S(2)}) copy-start(f32[10,7,128,128]{3,2,1,0:T(8,128)} %get-tuple-element.172) | copy-start | bytes 13762564
  94.5 23.2 %collective-permute-start.2 = (f32[3,7,128,128]{3,2,1,0:T(8,128)S(1)}, f32[3,7,128,128]{3,2,1,0:T(8,128)S(1)}, u32[]{:S(2)}, u32[]{:S(2)}) collective-permute-start(f32[3,7,128,128]{3,2,1,0:T(8,128)S(1)} %get-tuple-element.197), channel_id=1, source_target_pairs={{0,1},{1,2},{2,3},{3,4},{4,5},{5,6},{6,7},{7,8},{8,9},{9,10},{10,1... | collective-permute-start | bytes 4128776 | tf_op jit(solution)/shard_map/ppermute | solution.py:27
  94.6 23.4 %collective-permute-start.3 = (f32[3,7,128,128]{3,2,1,0:T(8,128)S(1)}, f32[3,7,128,128]{3,2,1,0:T(8,128)S(1)}, u32[]{:S(2)}, u32[]{:S(2)}) collective-permute-start(f32[3,7,128,128]{3,2,1,0:T(8,128)S(1)} %get-tuple-element.196), channel_id=1, source_target_pairs={{0,255},{1,0},{2,1},{3,2},{4,3},{5,4},{6,5},{7,6},{8,7},{9,8},{10,... | collective-permute-start | bytes 4128776 | tf_op jit(solution)/shard_map/ppermute | solution.py:27
  118.0 1.2 %copy-start.2 = (f32[4,7,128,128]{3,2,1,0:T(8,128)}, f32[4,7,128,128]{3,2,1,0:T(8,128)S(1)}, u32[]{:S(2)}) copy-start(f32[4,7,128,128]{3,2,1,0:T(8,128)S(1)} %add_dynamic-update-slice_fusion) | copy-start | bytes 5505028
where the time goes:
time: 123 us; the launch traced here: 122 us
  other arithmetic  31.4 us (26%)
  local copies, waits for them, and re-layouts  26.5 us (22%)
  waiting for transfers between devices  24.6 us (20%)
  matrix products  20.8 us (17%)
  starting transfers between devices  15.5 us (13%)
  loops' own time  2.97 us (2%)
    dot_general x20, matrix products, sign_density(): jnp.dot(rounded, square, preferred_element_type=jnp.float32)  20.8 us
    ppermute x2, waiting for transfers between devices, passed_along(): return lax.ppermute(value, axis, pairs)  15.8 us
    scatter-add x4, other arithmetic, visit(): accum = accum.at[local[:, None], slot].add(pieces)  13.9 us
    gather x4, local copies, waits for them, and re-layouts, visit(): blocks = padded[local[:, None], slot]  9.2 us
    ppermute x1, waiting for transfers between devices, extended(): lax.ppermute(lax.slice_in_dim(block, block.shape[dim] - width, None, axis...  8.83 us
    ppermute x1, starting transfers between devices, extended(): lax.ppermute(lax.slice_in_dim(block, 0, width, axis=dim), axis, backward)  8.21 us
    convert_element_type x4, other arithmetic, sign_density(): rounded = current.astype(jnp.bfloat16)  7.93 us
    ppermute x2, starting transfers between devices, passed_along(): return lax.ppermute(value, axis, pairs)  7.25 us
  transfers between devices with their start and end apart: 4, of which 2 were waited for; matrix products, arithmetic and copies ran while one was open for 0% of the time, Pallas kernels for 0%

commit v1 on v0

v1 whole, which is shorter than its diff:
```python
import jax
import jax.numpy as jnp
from jax import lax
from jax.experimental import pallas as pl
from jax.experimental.pallas import tpu as pltpu
from jax.sharding import PartitionSpec as P

B = 128
LIST = 4
W = 3
ITERS = 5
BAND = 7
ROWS = 4
EXT = ROWS + 2 * W
F32 = jnp.float32
BF16 = jnp.bfloat16
MESH = pl.DeviceIdType.MESH


def terms(row, col):
    low, high = min(row, col), max(row, col)
    return [z for z in range(ROWS) if z <= low and high <= z + 2 * W]


FAR = [(r, c) for r in range(W) for c in range(r + W + 1)]
NEAR = [(9 - r, 9 - c) for r, c in FAR]
FAR_SENDS = [[t for t in FAR if max(terms(*t)) == z] for z in range(W)]
NEAR_SENDS = [
    [t for t in NEAR if terms(*t) == [ROWS - 1]],
    [t for t in NEAR if terms(*t) != [ROWS - 1]],
]
STARTS = [0, 6, 11]
FAR_ORDER = sum(FAR_SENDS, [])
NEAR_ORDER = sum(NEAR_SENDS, [])


def kernel(
    lists, weights, scales, ham, owned, window, sym, xs, ys, qs, result,
    far_out, near_out, far_in, near_in,
    load_sem, halo_send, halo_recv, far_send, far_recv, near_send, near_recv,
):
    chip = lax.axis_index("blk")
    core = lax.axis_index("rep")
    chips = lax.axis_size("blk")
    total = ROWS * 2 * chips
    first = (chip * 2 + core) * ROWS
    near = (chip, 1 - core)
    far = (lax.rem(chip + 2 * core - 1 + chips, chips), 1 - core)

    def mirrored(value, last):
        return value + core * (last - 2 * value)

    load = pltpu.make_async_copy(ham, window.at[pl.ds(W, ROWS)], load_sem)
    load.start()
    barrier = pltpu.get_barrier_semaphore()
    for device in (near, far):
        pl.semaphore_signal(barrier, inc=1, device_id=device, device_id_type=MESH)

    position, place, share, member = [], [], [], []
    for z in range(ROWS):
        j = mirrored(z, ROWS - 1)
        spots = []
        for a in range(LIST):
            e = jnp.clip(lax.rem(lists[j, a] - first + W + total, total), 0, EXT - 1)
            spots.append(mirrored(e, EXT - 1))
        position.append(spots)
        places, shares, members = [], [], []
        for u in range(2 * W + 1):
            where = jnp.int32(0)
            weight = jnp.float32(0.0)
            here = jnp.float32(0.0)
            for a in range(LIST):
                hit = spots[a] == z + u
                where = jnp.where(hit, jnp.int32(a), where)
                weight = jnp.where(hit, weights[j, a], weight)
                here = jnp.where(hit, jnp.float32(1.0), here)
            places.append(where)
            shares.append(weight)
            members.append(here)
        place.append(places)
        share.append(shares)
        member.append(members)

    pl.semaphore_wait(barrier, 2)

    def halo(side, device, index):
        copies, arrivals = [], []
        for d in (1, 2, 3):
            count = BAND - d
            row = (1 - side) * (d - 1) + side * (ROWS - d)
            there = (1 - side) * (EXT - 1 - W + d) + side * (W - d)
            here = side * (EXT - 1 - W + d) + (1 - side) * (W - d)
            low = side * d
            low_here = (1 - side) * d
            copies.append(pltpu.make_async_remote_copy(
                src_ref=ham.at[row, pl.ds(low, count)],
                dst_ref=window.at[there, pl.ds(low, count)],
                send_sem=halo_send.at[index, d - 1],
                recv_sem=halo_recv.at[index, d - 1],
                device_id=device,
                device_id_type=MESH,
            ))
            arrivals.append(pltpu.make_async_remote_copy(
                src_ref=ham.at[row, pl.ds(low, count)],
                dst_ref=window.at[here, pl.ds(low_here, count)],
                send_sem=halo_send.at[index, d - 1],
                recv_sem=halo_recv.at[index, d - 1],
                device_id=device,
                device_id_type=MESH,
            ))
        return copies, arrivals

    far_copies, far_arrivals = halo(core, far, 0)
    near_copies, near_arrivals = halo(1 - core, near, 1)
    for d in range(W):
        near_copies[d].start()
        far_copies[d].start()

    def symmetrize(low, o):
        high = low + o
        slot = W + o * (1 - 2 * core)
        upper = window[mirrored(low, EXT - 1), slot]
        lower = window[mirrored(high, EXT - 1), 2 * W - slot]
        both = 0.5 * (upper.astype(F32) + lower.T.astype(F32))
        sym[low, W + o] = both
        if o:
            sym[high, W - o] = 0.5 * (lower.astype(F32) + upper.T.astype(F32))

    load.wait()
    for o in range(W + 1):
        for low in range(W, W + ROWS - o):
            symmetrize(low, o)
    for arrival in near_arrivals:
        arrival.wait_recv()
    for o in range(W + 1):
        for high in range(W + ROWS, EXT):
            symmetrize(high - o, o)

    diagonal = (
        lax.broadcasted_iota(jnp.int32, (B, B), 0) == lax.broadcasted_iota(jnp.int32, (B, B), 1)
    ).astype(F32)

    def assemble(z):
        j = mirrored(z, ROWS - 1)
        scale = scales[j]
        spots = []
        for a in range(LIST):
            e = jnp.clip(lax.rem(lists[j, a] - first + W + total, total), 0, EXT - 1)
            spots.append(mirrored(e, EXT - 1))
        for a in range(LIST):
            for b in range(LIST):
                offset = spots[b] - spots[a]
                stored = jnp.where(jnp.abs(offset) <= W, scale, jnp.float32(0.0))
                slot = jnp.clip(offset + W, 0, BAND - 1)
                block = stored * sym[spots[a], slot]
                xs[a * B : a * B + B, b * B : b * B + B] = block
                ys[0, a * B : a * B + B, b * B : b * B + B] = block.astype(BF16)

    def iterate(z):
        half = LIST * B // 2
        for k in range(ITERS):
            now, later = k % 2, (k + 1) % 2
            for m in range(0, LIST * B, half):
                qs[now, m : m + half, :] = jnp.dot(
                    ys[now, m : m + half, :], ys[now], preferred_element_type=F32
                ).astype(BF16)
            for m in range(0, LIST * B, half):
                value = 1.5 * xs[m : m + half, :] - 0.5 * jnp.dot(
                    ys[now, m : m + half, :], qs[now], preferred_element_type=F32
                )
                if k < ITERS - 1:
                    xs[m : m + half, :] = value
                    ys[later, m : m + half, :] = value.astype(BF16)
                    continue
                for a in range(m // B, (m + half) // B):
                    for b in range(LIST):
                        block = value[a * B - m : a * B - m + B, b * B : b * B + B]
                        if a == b:
                            result[z * LIST * LIST + a * LIST + b] = 0.5 * (diagonal - block)
                        else:
                            result[z * LIST * LIST + a * LIST + b] = -0.5 * block

    def gathered(row, col):
        value = None
        for z in terms(row, col):
            u, v = row - z, col - z
            factor = share[z][u] * member[z][v]
            term = factor * result[z * LIST * LIST + place[z][u] * LIST + place[z][v]]
            value = term if value is None else value + term
        return value

    def contribution(z):
        low, count = STARTS[z], len(FAR_SENDS[z])
        return pltpu.make_async_remote_copy(
            src_ref=far_out.at[pl.ds(low, count)],
            dst_ref=far_in.at[pl.ds(low, count)],
            send_sem=far_send.at[z],
            recv_sem=far_recv.at[z],
            device_id=far,
            device_id_type=MESH,
        )

    def near_contribution(i):
        low, count = i * len(NEAR_SENDS[0]), len(NEAR_SENDS[i])
        return pltpu.make_async_remote_copy(
            src_ref=near_out.at[pl.ds(low, count)],
            dst_ref=near_in.at[pl.ds(low, count)],
            send_sem=near_send.at[i],
            recv_sem=near_recv.at[i],
            device_id=near,
            device_id_type=MESH,
        )

    def send_far(z):
        for i, target in enumerate(FAR_SENDS[z]):
            far_out[STARTS[z] + i] = gathered(*target)
        contribution(z).start()

    def send_near(i):
        for n, target in enumerate(NEAR_SENDS[i]):
            near_out[i * len(NEAR_SENDS[0]) + n] = gathered(*target)
        near_contribution(i).start()

    def step(t, carry):
        z = lax.rem(t + ROWS - 1, ROWS)

        @pl.when(t == 1)
        def _():
            for arrival in far_arrivals:
                arrival.wait_recv()
            for o in range(W + 1):
                for low in range(W):
                    symmetrize(low, o)

        assemble(z)
        iterate(z)

        @pl.when(t == 0)
        def _():
            send_near(0)

        for sent in range(W):
            @pl.when(t == sent + 1)
            def _():
                send_far(sent)

        return carry

    lax.fori_loop(0, ROWS, step, 0)
    send_near(1)

    def spot(row, col):
        return mirrored(row - W, ROWS - 1), mirrored(col - row + W, BAND - 1)

    for row in range(W, W + ROWS):
        for col in range(row - W, row + W + 1):
            r, s = spot(row, col)
            owned[r, s] = gathered(row, col)

    def add_far(z):
        contribution(z).wait_recv()
        for i, (row, col) in enumerate(FAR_SENDS[z]):
            r, s = spot(5 - row, 5 - col)
            owned[r, s] += far_in[STARTS[z] + i]

    def add_near(i):
        near_contribution(i).wait_recv()
        for n, (row, col) in enumerate(NEAR_SENDS[i]):
            r, s = spot(13 - row, 13 - col)
            owned[r, s] += near_in[i * len(NEAR_SENDS[0]) + n]

    add_near(0)
    add_far(0)
    add_far(1)
    add_near(1)
    add_far(2)
    for d in range(W):
        near_copies[d].wait_send()
        far_copies[d].wait_send()
    for z in range(W):
        contribution(z).wait_send()
    for i in range(2):
        near_contribution(i).wait_send()


def on_device(hamiltonian, lists, scales, weights):
    smem = pl.BlockSpec(memory_space=pltpu.SMEM)
    hbm = pl.BlockSpec(memory_space=pl.ANY)
    operands = [
        pltpu.with_memory_space_constraint(value, pltpu.HBM)
        for value in (lists, weights, scales, hamiltonian)
    ]
    size = LIST * B
    return pl.pallas_call(
        kernel,
        name="density",
        out_shape=jax.ShapeDtypeStruct((ROWS, BAND, B, B), F32),
        in_specs=[smem, smem, smem, hbm],
        out_specs=pl.BlockSpec(memory_space=pltpu.VMEM),
        scratch_shapes=[
            pltpu.VMEM((EXT, BAND, B, B), BF16),
            pltpu.VMEM((EXT, BAND, B, B), F32),
            pltpu.VMEM((size, size), F32),
            pltpu.VMEM((2, size, size), BF16),
            pltpu.VMEM((2, size, size), BF16),
            pltpu.VMEM((ROWS * LIST * LIST, B, B), F32),
            pltpu.VMEM((len(FAR), B, B), F32),
            pltpu.VMEM((len(NEAR), B, B), F32),
            pltpu.VMEM((len(FAR), B, B), F32),
            pltpu.VMEM((len(NEAR), B, B), F32),
            pltpu.SemaphoreType.DMA,
            pltpu.SemaphoreType.DMA((2, W)),
            pltpu.SemaphoreType.DMA((2, W)),
            pltpu.SemaphoreType.DMA((W,)),
            pltpu.SemaphoreType.DMA((W,)),
            pltpu.SemaphoreType.DMA((2,)),
            pltpu.SemaphoreType.DMA((2,)),
        ],
        compiler_params=pltpu.CompilerParams(
            collective_id=0, has_side_effects=True, vmem_limit_bytes=40 << 20
        ),
    )(*operands)


def solution(mesh):
    in_specs = (
        P(("blk", "rep"), None, None, None),
        P(("blk", "rep"), None),
        P(("blk", "rep")),
        P(("blk", "rep"), None),
    )
    out_specs = P(("blk", "rep"), None, None, None)
    return jax.shard_map(
        on_device, mesh=mesh, in_specs=in_specs, out_specs=out_specs, check_vma=False
    )
```

time: 123 us -> 40.1 us (0.33)
  Pallas kernels: 0 us -> 38.8 us
  other arithmetic: 31.4 us -> 0 us
  local copies, waits for them, and re-layouts: 26.5 us -> 1.23 us
  waiting for transfers between devices: 24.6 us -> 0 us
  matrix products: 20.8 us -> 0 us
  starting transfers between devices: 15.5 us -> 0 us
  loops' own time: 2.97 us -> 0 us
    pallas_call x0 -> x1, Pallas kernels: none -> 38.8 us  [on_device(): pl.pallas_call(kernel, name='density', out_shape=jax.ShapeDtypeStruct((RO...]
    ppermute x4 -> x0, waiting for transfers between devices: 24.6 us -> none  [the longest x2 15.8 us: passed_along(): return lax.ppermute(value, axis, pairs)]
    dot_general x20 -> x0, matrix products: 20.8 us -> none  [sign_density(): jnp.dot(rounded, square, preferred_element_type=jnp.float32)]
    scatter-add x6 -> x0, other arithmetic: 16.7 us -> none  [the longest x4 13.9 us: visit(): accum = accum.at[local[:, None], slot].add(pieces)]
    ppermute x4 -> x0, starting transfers between devices: 15.5 us -> none  [the longest x1 8.21 us: extended(): lax.ppermute(lax.slice_in_dim(block, 0, width, axis=dim), axis, backward)]
    gather x4 -> x0, local copies, waits for them, and re-layouts: 9.2 us -> none  [visit(): blocks = padded[local[:, None], slot]]
    convert_element_type x8 -> x0, other arithmetic: 8.33 us -> none  [the longest x4 7.93 us: sign_density(): rounded = current.astype(jnp.bfloat16)]
    concatenate x13 -> x0, other arithmetic: 4.85 us -> none  [the longest x12 3.18 us: visit(): accum = accum.at[local[:, None], slot].add(pieces)]
  transfers between devices with their start and end apart: 4 -> 0, of which waited for: 2 -> 0; matrix products, arithmetic and copies ran while one was open for 0% -> 0% of each run, Pallas kernels for 0% -> 0%
where the time goes in v1:
time: 40.1 us; the launch traced here: 40 us
  Pallas kernels  38.8 us (97%)
  local copies, waits for them, and re-layouts  1.23 us (3%)
    pallas_call x1, Pallas kernels, on_device(): pl.pallas_call(kernel, name='density', out_shape=jax.ShapeDtypeStruct((RO...  38.8 us
    unnamed x1, local copies, waits for them, and re-layouts  1.23 us

profile of v1, /device:TPU:0, one launch (start us, length us, event | category | flops | bytes accessed | tf_op | source)
XLA Modules:
  0.0 40.0 jit_solution(15062242330678363189)
XLA Ops:
  0.0 38.8 %density.1 = f32[4,7,128,128]{3,2,1,0:T(8,128)S(1)} custom-call(s32[4,4]{1,0:T(4,128)} %lists.1, f32[4,4]{1,0:T(4,128)} %weights.1, f32[4]{0:T(128)} %scales.1, bf16[4,7,128,128]{3,2,1,0:T(8,128)(2,1)} %ham.1), custom_call_target="tpu_custom_call" | custom-call | tf_op jit(solution)/shard_map/density/pallas_call | solution.py:294
  38.8 1.2 %copy.6 = f32[4,7,128,128]{3,2,1,0:T(8,128)} copy(f32[4,7,128,128]{3,2,1,0:T(8,128)S(1)} %density.1) | data formatting | bytes 3670016

commit v2 on v1

v2 whole, which is shorter than its diff:
```python
import jax
import jax.numpy as jnp
from jax import lax
from jax.experimental import pallas as pl
from jax.experimental.pallas import tpu as pltpu
from jax.sharding import PartitionSpec as P

B = 128
LIST = 4
W = 3
ITERS = 5
BAND = 7
ROWS = 4
EXT = ROWS + 2 * W
F32 = jnp.float32
BF16 = jnp.bfloat16
MESH = pl.DeviceIdType.MESH


def terms(row, col):
    low, high = min(row, col), max(row, col)
    return [z for z in range(ROWS) if z <= low and high <= z + 2 * W]


FAR = [(r, c) for r in range(W) for c in range(r + W + 1)]
NEAR = [(9 - r, 9 - c) for r, c in FAR]
FAR_SENDS = [[t for t in FAR if max(terms(*t)) == z] for z in range(W)]
NEAR_SENDS = [
    [t for t in NEAR if terms(*t) == [ROWS - 1]],
    [t for t in NEAR if terms(*t) != [ROWS - 1]],
]
STARTS = [0, 6, 11]
EARLY = 3


def kernel(
    lists_hbm, weights_hbm, scales_hbm, ham, owned, lists, weights, scales, window, sym, xs, ys, qs, result,
    far_out, far_line_out, near_out, far_in, far_line_in, near_in,
    small_sem, load_sem, halo_send, halo_recv, far_send, far_recv, near_send, near_recv,
):
    chip = lax.axis_index("blk")
    core = lax.axis_index("rep")
    chips = lax.axis_size("blk")
    total = ROWS * 2 * chips
    first = (chip * 2 + core) * ROWS
    near = (chip, 1 - core)
    far = (lax.rem(chip + 2 * core - 1 + chips, chips), 1 - core)

    def mirrored(value, last):
        return value + core * (last - 2 * value)

    barrier = pltpu.get_barrier_semaphore()
    for device in (far, near):
        pl.semaphore_signal(barrier, inc=1, device_id=device, device_id_type=MESH)
    small = [
        pltpu.make_async_copy(source, target, small_sem.at[i])
        for i, (source, target) in enumerate(
            ((lists_hbm, lists), (weights_hbm, weights), (scales_hbm, scales))
        )
    ]
    for copy in small:
        copy.start()
    load = pltpu.make_async_copy(ham, window.at[pl.ds(W, ROWS)], load_sem)
    load.start()
    for copy in small:
        copy.wait()

    position, place, share, member = [], [], [], []
    for z in range(ROWS):
        j = mirrored(z, ROWS - 1)
        spots = []
        for a in range(LIST):
            e = jnp.clip(lax.rem(lists[j, a] - first + W + total, total), 0, EXT - 1)
            spots.append(mirrored(e, EXT - 1))
        position.append(spots)
        places, shares, members = [], [], []
        for u in range(2 * W + 1):
            where = jnp.int32(0)
            weight = jnp.float32(0.0)
            here = jnp.float32(0.0)
            for a in range(LIST):
                hit = spots[a] == z + u
                where = jnp.where(hit, jnp.int32(a), where)
                weight = jnp.where(hit, weights[j, a], weight)
                here = jnp.where(hit, jnp.float32(1.0), here)
            places.append(where)
            shares.append(weight)
            members.append(here)
        place.append(places)
        share.append(shares)
        member.append(members)

    pl.semaphore_wait(barrier, 2)

    far_runs = [[(2, 3, 4)], [(1, 3, 4), (2, 2, 1)], [(0, 3, 4), (1, 2, 1), (2, 1, 1)]]
    near_runs = [[(7, 0, 6), (8, 0, 5), (9, 0, 4)]]

    def halo(runs, device, corner, index):
        copies, arrivals = [], []
        for y, slot, count in runs:
            flipped = BAND - slot - count
            low = core * slot + (1 - core) * flipped
            low_here = (1 - core) * slot + core * flipped
            row = mirrored(corner - y, EXT - 1) - W
            there = core * y + (1 - core) * (EXT - 1 - y)
            for dst, source, kept in ((there, low, copies), (mirrored(y, EXT - 1), low_here, arrivals)):
                kept.append(pltpu.make_async_remote_copy(
                    src_ref=ham.at[row, pl.ds(source, count)],
                    dst_ref=window.at[dst, pl.ds(source, count)],
                    send_sem=halo_send.at[index],
                    recv_sem=halo_recv.at[index],
                    device_id=device,
                    device_id_type=MESH,
                ))
            index += 1
        return copies, arrivals

    near_copies, near_arrivals = halo(near_runs[0], near, 13, 0)
    far_copies, far_arrivals = [], []
    index = 3
    for runs in far_runs:
        copies, arrivals = halo(runs, far, 5, index)
        far_copies.append(copies)
        far_arrivals.append(arrivals)
        index += len(runs)
    for copy in near_copies + sum(far_copies, []):
        copy.start()

    def symmetrize(low, o):
        high = low + o
        slot = W + o * (1 - 2 * core)
        upper = window[mirrored(low, EXT - 1), slot]
        lower = window[mirrored(high, EXT - 1), 2 * W - slot]
        both = 0.5 * (upper.astype(F32) + lower.T.astype(F32))
        sym[low, W + o] = both
        if o:
            sym[high, W - o] = 0.5 * (lower.astype(F32) + upper.T.astype(F32))

    load.wait()
    for o in range(W + 1):
        for low in range(W, W + ROWS - o):
            symmetrize(low, o)
    for arrival in near_arrivals:
        arrival.wait_recv()
    for o in range(W + 1):
        for high in range(W + ROWS, EXT):
            symmetrize(high - o, o)

    on_diagonal = (
        lax.broadcasted_iota(jnp.int32, (B, B), 0) == lax.broadcasted_iota(jnp.int32, (B, B), 1)
    )
    diagonal = on_diagonal.astype(F32)
    size, half = LIST * B, LIST * B // 2

    def assemble(z):
        spots = position[z]
        scale = scales[mirrored(z, ROWS - 1)]
        for a in range(LIST):
            for b in range(LIST):
                offset = spots[b] - spots[a]
                stored = jnp.where(jnp.abs(offset) <= W, scale, jnp.float32(0.0))
                slot = jnp.clip(offset + W, 0, BAND - 1)
                block = stored * sym[spots[a], slot]
                xs[z, a * B : a * B + B, b * B : b * B + B] = block
                ys[z, 0, a * B : a * B + B, b * B : b * B + B] = block.astype(BF16)

    def iterate(z, steps):
        for k in steps:
            now, later = k % 2, (k + 1) % 2
            for m in range(0, size, half):
                qs[z, now, m : m + half, :] = jnp.dot(
                    ys[z, now, m : m + half, :], ys[z, now], preferred_element_type=F32
                ).astype(BF16)
            for m in range(0, size, half):
                value = 1.5 * xs[z, m : m + half, :] - 0.5 * jnp.dot(
                    ys[z, now, m : m + half, :], qs[z, now], preferred_element_type=F32
                )
                if k < ITERS - 1:
                    xs[z, m : m + half, :] = value
                    ys[z, later, m : m + half, :] = value.astype(BF16)
                    continue
                for a in range(m // B, (m + half) // B):
                    for b in range(LIST):
                        block = value[a * B - m : a * B - m + B, b * B : b * B + B]
                        if a == b:
                            result[z * LIST * LIST + a * LIST + b] = 0.5 * (diagonal - block)
                        else:
                            result[z * LIST * LIST + a * LIST + b] = -0.5 * block

    def gathered(row, col):
        value = None
        for z in terms(row, col):
            u, v = row - z, col - z
            factor = share[z][u] * member[z][v]
            term = factor * result[z * LIST * LIST + place[z][u] * LIST + place[z][v]]
            value = term if value is None else value + term
        return value

    def far_contributions(z):
        low, count = STARTS[z], len(FAR_SENDS[z])
        return [
            pltpu.make_async_remote_copy(
                src_ref=source,
                dst_ref=target,
                send_sem=far_send.at[z, i],
                recv_sem=far_recv.at[z, i],
                device_id=far,
                device_id_type=MESH,
            )
            for i, (source, target) in enumerate((
                (far_line_out.at[z], far_line_in.at[z]),
                (far_out.at[pl.ds(low, count)], far_in.at[pl.ds(low, count)]),
            ))
        ]

    def near_contribution(i):
        low, count = i * len(NEAR_SENDS[0]), len(NEAR_SENDS[i])
        return pltpu.make_async_remote_copy(
            src_ref=near_out.at[pl.ds(low, count)],
            dst_ref=near_in.at[pl.ds(low, count)],
            send_sem=near_send.at[i],
            recv_sem=near_recv.at[i],
            device_id=near,
            device_id_type=MESH,
        )

    def send_far(z):
        for i, target in enumerate(FAR_SENDS[z]):
            block = gathered(*target)
            if target == (z, z):
                line = jnp.sum(jnp.where(on_diagonal, block, 0.0), axis=0, keepdims=True)
                far_line_out[z] = jnp.broadcast_to(line, (8, B))
                block = jnp.where(on_diagonal, 0.0, block)
            far_out[STARTS[z] + i] = block.astype(BF16)
        for copy in far_contributions(z):
            copy.start()

    def send_near(i):
        for n, target in enumerate(NEAR_SENDS[i]):
            near_out[i * len(NEAR_SENDS[0]) + n] = gathered(*target)
        near_contribution(i).start()

    def far_halo(group):
        low = W - 1 - group
        for arrival in far_arrivals[group]:
            arrival.wait_recv()
        for o in range(W + 1):
            symmetrize(low, o)

    last = ROWS - 1
    assemble(last)
    iterate(last, range(ITERS))
    send_near(0)
    far_halo(0)
    assemble(2)
    iterate(2, range(EARLY))
    far_halo(1)
    far_halo(2)
    assemble(0)
    assemble(1)
    iterate(0, range(ITERS))
    send_far(0)
    iterate(1, range(ITERS))
    send_far(1)
    iterate(2, range(EARLY, ITERS))
    send_far(2)
    send_near(1)

    def spot(row, col):
        return mirrored(row - W, ROWS - 1), mirrored(col - row + W, BAND - 1)

    for row in range(W, W + ROWS):
        for col in range(row - W, row + W + 1):
            r, s = spot(row, col)
            owned[r, s] = gathered(row, col)

    def add_far(z):
        for copy in far_contributions(z):
            copy.wait_recv()
        for i, (row, col) in enumerate(FAR_SENDS[z]):
            block = far_in[STARTS[z] + i].astype(F32)
            if row == col:
                block = jnp.where(on_diagonal, far_line_in[z, 0:1, :], block)
            r, s = spot(5 - row, 5 - col)
            owned[r, s] += block

    def add_near(i):
        near_contribution(i).wait_recv()
        for n, (row, col) in enumerate(NEAR_SENDS[i]):
            r, s = spot(13 - row, 13 - col)
            owned[r, s] += near_in[i * len(NEAR_SENDS[0]) + n]

    add_near(0)
    add_far(0)
    add_far(1)
    add_near(1)
    add_far(2)
    for copy in near_copies + sum(far_copies, []):
        copy.wait_send()
    for z in range(W):
        for copy in far_contributions(z):
            copy.wait_send()
    for i in range(2):
        near_contribution(i).wait_send()


def on_device(hamiltonian, lists, scales, weights):
    hbm = pl.BlockSpec(memory_space=pl.ANY)
    operands = [
        pltpu.with_memory_space_constraint(value, pltpu.HBM)
        for value in (lists, weights, scales, hamiltonian)
    ]
    size = LIST * B
    return pl.pallas_call(
        kernel,
        name="density",
        out_shape=jax.ShapeDtypeStruct((ROWS, BAND, B, B), F32),
        in_specs=[hbm] * 4,
        out_specs=pl.BlockSpec(memory_space=pltpu.VMEM),
        scratch_shapes=[
            pltpu.SMEM((ROWS, LIST), jnp.int32),
            pltpu.SMEM((ROWS, LIST), F32),
            pltpu.SMEM((ROWS,), F32),
            pltpu.VMEM((EXT, BAND, B, B), BF16),
            pltpu.VMEM((EXT, BAND, B, B), F32),
            pltpu.VMEM((ROWS, size, size), F32),
            pltpu.VMEM((ROWS, 2, size, size), BF16),
            pltpu.VMEM((ROWS, 2, size, size), BF16),
            pltpu.VMEM((ROWS * LIST * LIST, B, B), F32),
            pltpu.VMEM((len(FAR), B, B), BF16),
            pltpu.VMEM((W, 8, B), F32),
            pltpu.VMEM((len(NEAR), B, B), F32),
            pltpu.VMEM((len(FAR), B, B), BF16),
            pltpu.VMEM((W, 8, B), F32),
            pltpu.VMEM((len(NEAR), B, B), F32),
            pltpu.SemaphoreType.DMA((3,)),
            pltpu.SemaphoreType.DMA,
            pltpu.SemaphoreType.DMA((9,)),
            pltpu.SemaphoreType.DMA((9,)),
            pltpu.SemaphoreType.DMA((W, 2)),
            pltpu.SemaphoreType.DMA((W, 2)),
            pltpu.SemaphoreType.DMA((2,)),
            pltpu.SemaphoreType.DMA((2,)),
        ],
        compiler_params=pltpu.CompilerParams(
            collective_id=0, has_side_effects=True, vmem_limit_bytes=40 << 20
        ),
    )(*operands)


def solution(mesh):
    in_specs = (
        P(("blk", "rep"), None, None, None),
        P(("blk", "rep"), None),
        P(("blk", "rep")),
        P(("blk", "rep"), None),
    )
    out_specs = P(("blk", "rep"), None, None, None)
    return jax.shard_map(
        on_device, mesh=mesh, in_specs=in_specs, out_specs=out_specs, check_vma=False
    )
```

time: 40.1 us -> 35.8 us (0.89)
  Pallas kernels: 38.8 us -> 34.4 us
    pallas_call x1, Pallas kernels: 38.8 us -> 34.4 us  [on_device(): pl.pallas_call(kernel, name='density', out_shape=jax.ShapeDtypeStruct((RO...]
where the time goes in v2:
time: 35.8 us; the launch traced here: 35.7 us
  Pallas kernels  34.4 us (96%)
  local copies, waits for them, and re-layouts  1.23 us (3%)
    pallas_call x1, Pallas kernels, on_device(): pl.pallas_call(kernel, name='density', out_shape=jax.ShapeDtypeStruct((RO...  34.4 us
    unnamed x1, local copies, waits for them, and re-layouts  1.23 us

profile of v2, /device:TPU:0, one launch (start us, length us, event | category | flops | bytes accessed | tf_op | source)
XLA Modules:
  0.0 35.7 jit_solution(4852541818679683112)
XLA Ops:
  0.0 34.4 %density.1 = f32[4,7,128,128]{3,2,1,0:T(8,128)S(1)} custom-call(s32[4,4]{1,0:T(4,128)} %lists_hbm.1, f32[4,4]{1,0:T(4,128)} %weights_hbm.1, f32[4]{0:T(128)} %scales_hbm.1, bf16[4,7,128,128]{3,2,1,0:T(8,128)(2,1)} %ham.1), custom_call_target="tpu_custom_call" | custom-call | tf_op jit(solution)/shard_map/density/pallas_call | solution.py:314
  34.4 1.2 %copy.6 = f32[4,7,128,128]{3,2,1,0:T(8,128)} copy(f32[4,7,128,128]{3,2,1,0:T(8,128)S(1)} %density.1) | data formatting | bytes 3670016

commit v3 on v2

--- a/solution.py
+++ b/solution.py
@@ -30,13 +30,14 @@
     [t for t in NEAR if terms(*t) != [ROWS - 1]],
 ]
 STARTS = [0, 6, 11]
+MIRRORED = [(a, b) for a in range(LIST // 2, LIST) for b in range(LIST // 2)]
 EARLY = 3
 
 
 def kernel(
     lists_hbm, weights_hbm, scales_hbm, ham, owned, lists, weights, scales, window, sym, xs, ys, qs, result,
     far_out, far_line_out, near_out, far_in, far_line_in, near_in,
-    small_sem, load_sem, halo_send, halo_recv, far_send, far_recv, near_send, near_recv,
+    ready, small_sem, load_sem, halo_send, halo_recv, far_send, far_recv, near_send, near_recv,
 ):
     chip = lax.axis_index("blk")
     core = lax.axis_index("rep")
@@ -90,7 +91,14 @@
         share.append(shares)
         member.append(members)
 
-    pl.semaphore_wait(barrier, 2)
+    @pl.when(core == 1)
+    def _():
+        pl.semaphore_wait(barrier, 2)
+        pl.semaphore_signal(ready, inc=1, device_id=near, device_id_type=MESH)
+
+    @pl.when(core == 0)
+    def _():
+        pl.semaphore_wait(ready, 1)
 
     far_runs = [[(2, 3, 4)], [(1, 3, 4), (2, 2, 1)], [(0, 3, 4), (1, 2, 1), (2, 1, 1)]]
     near_runs = [[(7, 0, 6), (8, 0, 5), (9, 0, 4)]]
@@ -123,7 +131,14 @@
         far_copies.append(copies)
         far_arrivals.append(arrivals)
         index += len(runs)
-    for copy in near_copies + sum(far_copies, []):
+    for copy in near_copies:
+        copy.start()
+
+    @pl.when(core == 0)
+    def _():
+        pl.semaphore_wait(barrier, 2)
+
+    for copy in sum(far_copies, []):
         copy.start()
 
     def symmetrize(low, o):
@@ -161,31 +176,43 @@
                 stored = jnp.where(jnp.abs(offset) <= W, scale, jnp.float32(0.0))
                 slot = jnp.clip(offset + W, 0, BAND - 1)
                 block = stored * sym[spots[a], slot]
-                xs[z, a * B : a * B + B, b * B : b * B + B] = block
+                if (a, b) not in MIRRORED:
+                    xs[z, a * B : a * B + B, b * B : b * B + B] = block
                 ys[z, 0, a * B : a * B + B, b * B : b * B + B] = block.astype(BF16)
 
+    low, high, whole = slice(0, half), slice(half, size), slice(0, size)
+    quarters = ((low, high), (high, high), (low, low))
+
     def iterate(z, steps):
+        base = z * LIST * LIST
         for k in steps:
             now, later = k % 2, (k + 1) % 2
-            for m in range(0, size, half):
-                qs[z, now, m : m + half, :] = jnp.dot(
-                    ys[z, now, m : m + half, :], ys[z, now], preferred_element_type=F32
+            for rows, cols in quarters:
+                square = jnp.dot(
+                    ys[z, now, rows, whole], ys[z, now, whole, cols], preferred_element_type=F32
                 ).astype(BF16)
-            for m in range(0, size, half):
-                value = 1.5 * xs[z, m : m + half, :] - 0.5 * jnp.dot(
-                    ys[z, now, m : m + half, :], qs[z, now], preferred_element_type=F32
+                qs[z, now, rows, cols] = square
+                if rows != cols:
+                    qs[z, now, cols, rows] = square.T
+            for rows, cols in quarters:
+                value = 1.5 * xs[z, rows, cols] - 0.5 * jnp.dot(
+                    ys[z, now, rows, whole], qs[z, now, whole, cols], preferred_element_type=F32
                 )
                 if k < ITERS - 1:
-                    xs[z, m : m + half, :] = value
-                    ys[z, later, m : m + half, :] = value.astype(BF16)
+                    xs[z, rows, cols] = value
+                    rounded = value.astype(BF16)
+                    ys[z, later, rows, cols] = rounded
+                    if rows != cols:
+                        ys[z, later, cols, rows] = rounded.T
                     continue
-                for a in range(m // B, (m + half) // B):
-                    for b in range(LIST):
-                        block = value[a * B - m : a * B - m + B, b * B : b * B + B]
-                        if a == b:
-                            result[z * LIST * LIST + a * LIST + b] = 0.5 * (diagonal - block)
-                        else:
-                            result[z * LIST * LIST + a * LIST + b] = -0.5 * block
+                for m in range(LIST // 2):
+                    for n in range(LIST // 2):
+                        a, b = rows.start // B + m, cols.start // B + n
+                        block = value[m * B : m * B + B, n * B : n * B + B]
+                        block = 0.5 * (diagonal - block) if a == b else -0.5 * block
+                        result[base + a * LIST + b] = block
+                        if rows != cols:
+                            result[base + b * LIST + a] = block.T
 
     def gathered(row, col):
         value = None
@@ -255,12 +282,13 @@
     assemble(2)
     iterate(2, range(EARLY))
     far_halo(1)
+    assemble(1)
+    iterate(1, range(2))
     far_halo(2)
     assemble(0)
-    assemble(1)
     iterate(0, range(ITERS))
     send_far(0)
-    iterate(1, range(ITERS))
+    iterate(1, range(2, ITERS))
     send_far(1)
     iterate(2, range(EARLY, ITERS))
     send_far(2)
@@ -333,6 +361,7 @@
             pltpu.VMEM((len(FAR), B, B), BF16),
             pltpu.VMEM((W, 8, B), F32),
             pltpu.VMEM((len(NEAR), B, B), F32),
+            pltpu.SemaphoreType.REGULAR,
             pltpu.SemaphoreType.DMA((3,)),
             pltpu.SemaphoreType.DMA,
             pltpu.SemaphoreType.DMA((9,)),

time: 35.8 us -> 33.7 us (0.941)
  Pallas kernels: 34.4 us -> 32.4 us
    pallas_call x1, Pallas kernels: 34.4 us -> 32.4 us  [on_device(): pl.pallas_call(kernel, name='density', out_shape=jax.ShapeDtypeStruct((RO...]
where the time goes in v3:
time: 33.7 us; the launch traced here: 33.6 us
  Pallas kernels  32.4 us (96%)
  local copies, waits for them, and re-layouts  1.23 us (4%)
    pallas_call x1, Pallas kernels, on_device(): pl.pallas_call(kernel, name='density', out_shape=jax.ShapeDtypeStruct((RO...  32.4 us
    unnamed x1, local copies, waits for them, and re-layouts  1.23 us

profile of v3, /device:TPU:0, one launch (start us, length us, event | category | flops | bytes accessed | tf_op | source)
XLA Modules:
  0.0 33.6 jit_solution(18295354911315687140)
XLA Ops:
  0.0 32.4 %density.1 = f32[4,7,128,128]{3,2,1,0:T(8,128)S(1)} custom-call(s32[4,4]{1,0:T(4,128)} %lists_hbm.1, f32[4,4]{1,0:T(4,128)} %weights_hbm.1, f32[4]{0:T(128)} %scales_hbm.1, bf16[4,7,128,128]{3,2,1,0:T(8,128)(2,1)} %ham.1), custom_call_target="tpu_custom_call" | custom-call | tf_op jit(solution)/shard_map/density/pallas_call | solution.py:342
  32.4 1.2 %copy.6 = f32[4,7,128,128]{3,2,1,0:T(8,128)} copy(f32[4,7,128,128]{3,2,1,0:T(8,128)S(1)} %density.1) | data formatting | bytes 3670016

commit v4 on v3

--- a/solution.py
+++ b/solution.py
@@ -29,7 +29,10 @@
     [t for t in NEAR if terms(*t) == [ROWS - 1]],
     [t for t in NEAR if terms(*t) != [ROWS - 1]],
 ]
-STARTS = [0, 6, 11]
+FAR_SENDS[0] = [(0, 0), (0, 3), (0, 1), (0, 2)]
+SHARED = [(0, 1), (0, 2)]
+STARTS = [0, 4, 9]
+FAR_BLOCKS = 13
 MIRRORED = [(a, b) for a in range(LIST // 2, LIST) for b in range(LIST // 2)]
 EARLY = 3
 
@@ -224,7 +227,8 @@
         return value
 
     def far_contributions(z):
-        low, count = STARTS[z], len(FAR_SENDS[z])
+        ends = [0, 2, 4] if z == 0 else [0, len(FAR_SENDS[z])]
+        runs = [pl.ds(STARTS[z] + low, high - low) for low, high in zip(ends, ends[1:])]
         return [
             pltpu.make_async_remote_copy(
                 src_ref=source,
@@ -234,10 +238,10 @@
                 device_id=far,
                 device_id_type=MESH,
             )
-            for i, (source, target) in enumerate((
-                (far_line_out.at[z], far_line_in.at[z]),
-                (far_out.at[pl.ds(low, count)], far_in.at[pl.ds(low, count)]),
-            ))
+            for i, (source, target) in enumerate(
+                [(far_line_out.at[z], far_line_in.at[z])]
+                + [(far_out.at[run], far_in.at[run]) for run in runs]
+            )
         ]
 
     def near_contribution(i):
@@ -252,15 +256,28 @@
         )
 
     def send_far(z):
+        copies = far_contributions(z)
         for i, target in enumerate(FAR_SENDS[z]):
-            block = gathered(*target)
+            if target in SHARED:
+                u, v = target
+                factor = member[z][u] * member[z][v]
+                block = factor * result[z * LIST * LIST + place[z][u] * LIST + place[z][v]]
+            else:
+                block = gathered(*target)
             if target == (z, z):
                 line = jnp.sum(jnp.where(on_diagonal, block, 0.0), axis=0, keepdims=True)
-                far_line_out[z] = jnp.broadcast_to(line, (8, B))
+                lines = jnp.broadcast_to(line, (8, B))
+                if z == 0:
+                    row = lax.broadcasted_iota(jnp.int32, (8, B), 0)
+                    for u in range(W):
+                        lines = jnp.where(row == u + 1, share[z][u], lines)
+                far_line_out[z] = lines
                 block = jnp.where(on_diagonal, 0.0, block)
             far_out[STARTS[z] + i] = block.astype(BF16)
-        for copy in far_contributions(z):
-            copy.start()
+            if z == 0 and i == 1:
+                copies[1].start()
+        copies[-1].start()
+        copies[0].start()
 
     def send_near(i):
         for n, target in enumerate(NEAR_SENDS[i]):
@@ -283,12 +300,12 @@
     iterate(2, range(EARLY))
     far_halo(1)
     assemble(1)
-    iterate(1, range(2))
+    iterate(1, range(3))
     far_halo(2)
     assemble(0)
     iterate(0, range(ITERS))
     send_far(0)
-    iterate(1, range(2, ITERS))
+    iterate(1, range(3, ITERS))
     send_far(1)
     iterate(2, range(EARLY, ITERS))
     send_far(2)
@@ -307,6 +324,10 @@
             copy.wait_recv()
         for i, (row, col) in enumerate(FAR_SENDS[z]):
             block = far_in[STARTS[z] + i].astype(F32)
+            if (row, col) in SHARED:
+                r, s = spot(5 - col, 5 - row)
+                owned[r, s] += far_line_in[z, 1 + col : 2 + col, :] * block.T
+                block = far_line_in[z, 1 + row : 2 + row, :] * block
             if row == col:
                 block = jnp.where(on_diagonal, far_line_in[z, 0:1, :], block)
             r, s = spot(5 - row, 5 - col)
@@ -355,10 +376,10 @@
             pltpu.VMEM((ROWS, 2, size, size), BF16),
             pltpu.VMEM((ROWS, 2, size, size), BF16),
             pltpu.VMEM((ROWS * LIST * LIST, B, B), F32),
-            pltpu.VMEM((len(FAR), B, B), BF16),
+            pltpu.VMEM((FAR_BLOCKS, B, B), BF16),
             pltpu.VMEM((W, 8, B), F32),
             pltpu.VMEM((len(NEAR), B, B), F32),
-            pltpu.VMEM((len(FAR), B, B), BF16),
+            pltpu.VMEM((FAR_BLOCKS, B, B), BF16),
             pltpu.VMEM((W, 8, B), F32),
             pltpu.VMEM((len(NEAR), B, B), F32),
             pltpu.SemaphoreType.REGULAR,
@@ -366,8 +387,8 @@
             pltpu.SemaphoreType.DMA,
             pltpu.SemaphoreType.DMA((9,)),
             pltpu.SemaphoreType.DMA((9,)),
-            pltpu.SemaphoreType.DMA((W, 2)),
-            pltpu.SemaphoreType.DMA((W, 2)),
+            pltpu.SemaphoreType.DMA((W, W)),
+            pltpu.SemaphoreType.DMA((W, W)),
             pltpu.SemaphoreType.DMA((2,)),
             pltpu.SemaphoreType.DMA((2,)),
         ],

time: 33.7 us -> 33.3 us (0.988)
  Pallas kernels: 32.4 us -> 32 us
    pallas_call x1, Pallas kernels: 32.4 us -> 32 us  [on_device(): pl.pallas_call(kernel, name='density', out_shape=jax.ShapeDtypeStruct((RO...]
where the time goes in v4:
time: 33.3 us; the launch traced here: 33.2 us
  Pallas kernels  32 us (96%)
  local copies, waits for them, and re-layouts  1.23 us (4%)
    pallas_call x1, Pallas kernels, on_device(): pl.pallas_call(kernel, name='density', out_shape=jax.ShapeDtypeStruct((RO...  32 us
    unnamed x1, local copies, waits for them, and re-layouts  1.23 us

profile of v4, /device:TPU:0, one launch (start us, length us, event | category | flops | bytes accessed | tf_op | source)
XLA Modules:
  0.0 33.2 jit_solution(11089271506939800007)
XLA Ops:
  0.0 32.0 %density.1 = f32[4,7,128,128]{3,2,1,0:T(8,128)S(1)} custom-call(s32[4,4]{1,0:T(4,128)} %lists_hbm.1, f32[4,4]{1,0:T(4,128)} %weights_hbm.1, f32[4]{0:T(128)} %scales_hbm.1, bf16[4,7,128,128]{3,2,1,0:T(8,128)(2,1)} %ham.1), custom_call_target="tpu_custom_call" | custom-call | tf_op jit(solution)/shard_map/density/pallas_call | solution.py:363
  32.0 1.2 %copy.6 = f32[4,7,128,128]{3,2,1,0:T(8,128)} copy(f32[4,7,128,128]{3,2,1,0:T(8,128)S(1)} %density.1) | data formatting | bytes 3670016

commit v5 on v4

--- a/solution.py
+++ b/solution.py
@@ -34,7 +34,7 @@
 STARTS = [0, 4, 9]
 FAR_BLOCKS = 13
 MIRRORED = [(a, b) for a in range(LIST // 2, LIST) for b in range(LIST // 2)]
-EARLY = 3
+EARLY = 4
 
 
 def kernel(
@@ -134,15 +134,19 @@
         far_copies.append(copies)
         far_arrivals.append(arrivals)
         index += len(runs)
-    for copy in near_copies:
-        copy.start()
+    @pl.when(core == 1)
+    def _():
+        for copy in sum(far_copies, []) + near_copies:
+            copy.start()
 
     @pl.when(core == 0)
     def _():
+        for copy in near_copies:
+            copy.start()
         pl.semaphore_wait(barrier, 2)
-
-    for copy in sum(far_copies, []):
-        copy.start()
+        for copy in sum(far_copies, []):
+            copy.start()
+
 
     def symmetrize(low, o):
         high = low + o
@@ -190,7 +194,7 @@
         base = z * LIST * LIST
         for k in steps:
             now, later = k % 2, (k + 1) % 2
-            for rows, cols in quarters:
+            for rows, cols in (quarters[1], quarters[0], quarters[2]):
                 square = jnp.dot(
                     ys[z, now, rows, whole], ys[z, now, whole, cols], preferred_element_type=F32
                 ).astype(BF16)

time: 33.3 us -> 34 us (1.021)
  Pallas kernels: 32 us -> 32.7 us
    pallas_call x1, Pallas kernels: 32 us -> 32.7 us  [on_device(): pl.pallas_call(kernel, name='density', out_shape=jax.ShapeDtypeStruct((RO...]
where the time goes in v5:
time: 34 us; the launch traced here: 33.9 us
  Pallas kernels  32.7 us (96%)
  local copies, waits for them, and re-layouts  1.23 us (4%)
    pallas_call x1, Pallas kernels, on_device(): pl.pallas_call(kernel, name='density', out_shape=jax.ShapeDtypeStruct((RO...  32.7 us
    unnamed x1, local copies, waits for them, and re-layouts  1.23 us

profile of v5, /device:TPU:0, one launch (start us, length us, event | category | flops | bytes accessed | tf_op | source)
XLA Modules:
  0.0 33.9 jit_solution(4619184493378356735)
XLA Ops:
  0.0 32.7 %density.1 = f32[4,7,128,128]{3,2,1,0:T(8,128)S(1)} custom-call(s32[4,4]{1,0:T(4,128)} %lists_hbm.1, f32[4,4]{1,0:T(4,128)} %weights_hbm.1, f32[4]{0:T(128)} %scales_hbm.1, bf16[4,7,128,128]{3,2,1,0:T(8,128)(2,1)} %ham.1), custom_call_target="tpu_custom_call" | custom-call | tf_op jit(solution)/shard_map/density/pallas_call | solution.py:367
  32.7 1.2 %copy.6 = f32[4,7,128,128]{3,2,1,0:T(8,128)} copy(f32[4,7,128,128]{3,2,1,0:T(8,128)S(1)} %density.1) | data formatting | bytes 3670016

commit v6 on v5

--- a/solution.py
+++ b/solution.py
@@ -34,7 +34,7 @@
 STARTS = [0, 4, 9]
 FAR_BLOCKS = 13
 MIRRORED = [(a, b) for a in range(LIST // 2, LIST) for b in range(LIST // 2)]
-EARLY = 4
+EARLY = 3
 
 
 def kernel(
@@ -298,7 +298,6 @@
     last = ROWS - 1
     assemble(last)
     iterate(last, range(ITERS))
-    send_near(0)
     far_halo(0)
     assemble(2)
     iterate(2, range(EARLY))
@@ -314,6 +313,7 @@
     iterate(2, range(EARLY, ITERS))
     send_far(2)
     send_near(1)
+    send_near(0)
 
     def spot(row, col):
         return mirrored(row - W, ROWS - 1), mirrored(col - row + W, BAND - 1)
@@ -343,10 +343,10 @@
             r, s = spot(13 - row, 13 - col)
             owned[r, s] += near_in[i * len(NEAR_SENDS[0]) + n]
 
-    add_near(0)
     add_far(0)
     add_far(1)
     add_near(1)
+    add_near(0)
     add_far(2)
     for copy in near_copies + sum(far_copies, []):
         copy.wait_send()

time: 34 us -> 33.4 us (0.982)
  Pallas kernels: 32.7 us -> 32.1 us
    pallas_call x1, Pallas kernels: 32.7 us -> 32.1 us  [on_device(): pl.pallas_call(kernel, name='density', out_shape=jax.ShapeDtypeStruct((RO...]
where the time goes in v6:
time: 33.4 us; the launch traced here: 33.3 us
  Pallas kernels  32.1 us (96%)
  local copies, waits for them, and re-layouts  1.23 us (4%)
    pallas_call x1, Pallas kernels, on_device(): pl.pallas_call(kernel, name='density', out_shape=jax.ShapeDtypeStruct((RO...  32.1 us
    unnamed x1, local copies, waits for them, and re-layouts  1.23 us

profile of v6, /device:TPU:0, one launch (start us, length us, event | category | flops | bytes accessed | tf_op | source)
XLA Modules:
  0.0 33.3 jit_solution(11663368519126048569)
XLA Ops:
  0.0 32.1 %density.1 = f32[4,7,128,128]{3,2,1,0:T(8,128)S(1)} custom-call(s32[4,4]{1,0:T(4,128)} %lists_hbm.1, f32[4,4]{1,0:T(4,128)} %weights_hbm.1, f32[4]{0:T(128)} %scales_hbm.1, bf16[4,7,128,128]{3,2,1,0:T(8,128)(2,1)} %ham.1), custom_call_target="tpu_custom_call" | custom-call | tf_op jit(solution)/shard_map/density/pallas_call | solution.py:367
  32.1 1.2 %copy.6 = f32[4,7,128,128]{3,2,1,0:T(8,128)} copy(f32[4,7,128,128]{3,2,1,0:T(8,128)S(1)} %density.1) | data formatting | bytes 3670016
